TPU v7x, 256 devices: a whole 4x4x8 slice. The times are simulated.
256 devices in a mesh: worker: 16 (over y, z_lo, core), expert: 16 (over z_hi, x).
Axes of the slice: x: 4, y: 4, z: 8 (z_hi: 4, z_lo: 2; z = z_hi * 2 + z_lo), core: 2. Of those that a mesh axis runs over, the one named last changes fastest.
Arguments:
- tokens: bfloat16 [32768, 3072], P(('worker', 'expert')), may hold values from -6 to 6
- route_ids: int32 [32768, 2], P(('worker', 'expert')), may hold values from 0 to 3, as said below
- route_mix: float32 [32768, 2], P(('worker', 'expert')), may hold values from 0.1 to 1
- target: bfloat16 [32768, 3072], P(('worker', 'expert')), may hold values from -6 to 6
- step_count: int32 [16], P('worker'), may hold values from 8 to 101
- gate_weight: bfloat16 [3072, 4096], P(None, 'expert'), may hold values from -0.109375 to 0.109375
- up_weight: bfloat16 [3072, 4096], P(None, 'expert'), may hold values from -0.109375 to 0.109375
- down_weight: bfloat16 [4096, 3072], P('expert'), may hold values from -0.1875 to 0.1875
Outputs:
- outer_gate: float32 [3072, 4096], P('worker', 'expert')
- outer_up: float32 [3072, 4096], P('worker', 'expert')
- outer_down: float32 [4096, 3072], P('expert', 'worker')
- token_loss: float32 [32768], P(('worker', 'expert'))
Inputs may be any that keep to these rules, and one draw needn't show every extreme that they name: `route_ids`: each token's 2 experts differ. In the 128 rows of one device no expert is named by more than 80 rows, and in every device's rows some expert is named by exactly 80.
All inputs are finite; a program needn't handle non-finite values.
Results may differ from a plain program's by a relative error of at most 0.017.
Values may be sent and summed in bfloat16 or wider, within the bound.
A program may use at most 128 MiB of HBM per device.

v0:
```python
import jax
import jax.numpy as jnp
from jax import lax
from jax.sharding import PartitionSpec as P

EXPERTS = 4
CAP = 80


def silu_parts(pre):
    sigmoid_val = jax.nn.sigmoid(pre)
    return (pre * sigmoid_val, sigmoid_val * (1.0 + pre * (1.0 - sigmoid_val)))


def contract_rows(left, right):
    return lax.dot_general(
        left, right, (((0,), (0,)), ((), ())), preferred_element_type=jnp.float32
    )


def expert_forward(inputs, gate_weight, up_weight, down_weight):
    gate_pre = jnp.dot(inputs, gate_weight, preferred_element_type=jnp.float32)
    up_pre = jnp.dot(inputs, up_weight, preferred_element_type=jnp.float32)
    hidden = (gate_pre * jax.nn.sigmoid(gate_pre) * up_pre).astype(jnp.bfloat16)
    partial_out = jnp.dot(hidden, down_weight, preferred_element_type=jnp.float32).astype(
        jnp.bfloat16
    )
    return (gate_pre, up_pre, hidden, partial_out)


def hidden_grads(cotangent, gate_pre, up_pre, down_weight):
    grad_hidden = lax.dot_general(
        cotangent, down_weight, (((1,), (1,)), ((), ())), preferred_element_type=jnp.float32
    )
    activated, slope = silu_parts(gate_pre)
    return (
        (grad_hidden * up_pre * slope).astype(jnp.bfloat16),
        (grad_hidden * activated).astype(jnp.bfloat16),
    )


def per_device(
    tokens, route_ids, route_mix, target, step_count, gate_weight, up_weight, down_weight
):
    tok_dev, width = tokens.shape
    topk = route_ids.shape[1]
    route_total = tok_dev * topk
    expert_devices = lax.axis_size("expert")
    hsplit = expert_devices // EXPERTS
    slot_total = expert_devices * CAP
    flat_ids = route_ids.reshape(-1)
    expert_hit = (flat_ids[:, None] == jnp.arange(EXPERTS, dtype=jnp.int32)[None, :]).astype(
        jnp.int32
    )
    earlier = jnp.cumsum(expert_hit, axis=0) - expert_hit
    slot_index = jnp.sum(earlier * expert_hit, axis=1)
    slot_key = flat_ids * CAP + slot_index
    route_of_slot = (
        jnp.full((EXPERTS * CAP,), route_total, jnp.int32)
        .at[slot_key]
        .set(jnp.arange(route_total, dtype=jnp.int32))
    )
    send_live = route_of_slot < route_total
    safe_route = jnp.minimum(route_of_slot, route_total - 1)
    token_picked = jnp.take(tokens, safe_route // topk, axis=0)
    dispatch_one = jnp.where(
        send_live[:, None], token_picked, jnp.zeros_like(token_picked)
    ).reshape(EXPERTS, CAP, width)
    send_tokens = jnp.broadcast_to(dispatch_one[:, None], (EXPERTS, hsplit, CAP, width)).reshape(
        expert_devices, CAP, width
    )
    arrived = lax.all_to_all(send_tokens, "expert", split_axis=0, concat_axis=0, tiled=True)
    expert_rows = arrived.reshape(slot_total, width)
    gate_pre, up_pre, hidden, partial_slots = expert_forward(
        expert_rows, gate_weight, up_weight, down_weight
    )
    returned = lax.all_to_all(
        partial_slots.reshape(expert_devices, CAP, width),
        "expert",
        split_axis=0,
        concat_axis=0,
        tiled=True,
    )
    expert_out = jnp.sum(
        returned.reshape(EXPERTS, hsplit, CAP, width).astype(jnp.float32), axis=1
    ).reshape(EXPERTS * CAP, width)
    picked_rows = jnp.take(expert_out, slot_key, axis=0).reshape(tok_dev, topk, width)
    mixed_out = jnp.sum(route_mix[:, :, None] * picked_rows, axis=1)
    residual = mixed_out - target.astype(jnp.float32)
    token_loss = 0.5 * jnp.mean(residual * residual, axis=1)
    cot_routes = (
        (route_mix[:, :, None] * residual[:, None, :])
        .astype(jnp.bfloat16)
        .reshape(route_total, width)
    )
    cot_picked = jnp.take(cot_routes, safe_route, axis=0)
    cot_one = jnp.where(send_live[:, None], cot_picked, jnp.zeros_like(cot_picked)).reshape(
        EXPERTS, CAP, width
    )
    send_cot = jnp.broadcast_to(cot_one[:, None], (EXPERTS, hsplit, CAP, width)).reshape(
        expert_devices, CAP, width
    )
    cot_arrived = lax.all_to_all(send_cot, "expert", split_axis=0, concat_axis=0, tiled=True)
    cot_slots = cot_arrived.reshape(slot_total, width)
    weight = step_count[0].astype(jnp.float32)
    total_steps = lax.psum(weight, "worker")
    grad_gate, grad_up = hidden_grads(cot_slots, gate_pre, up_pre, down_weight)
    down_grad, grad_gate, grad_up = (contract_rows(hidden, cot_slots), grad_gate, grad_up)
    gate_grad = contract_rows(expert_rows, grad_gate)
    up_grad = contract_rows(expert_rows, grad_up)
    outer_gate, outer_up, outer_down = (
        lax.psum_scatter(
            (weight * gate_grad).astype(jnp.bfloat16), "worker", scatter_dimension=0, tiled=True
        ).astype(jnp.float32),
        lax.psum_scatter(
            (weight * up_grad).astype(jnp.bfloat16), "worker", scatter_dimension=0, tiled=True
        ).astype(jnp.float32),
        lax.psum_scatter(
            (weight * down_grad).astype(jnp.bfloat16), "worker", scatter_dimension=1, tiled=True
        ).astype(jnp.float32),
    )
    return (outer_gate / total_steps, outer_up / total_steps, outer_down / total_steps, token_loss)


def solution(mesh):
    return jax.shard_map(
        per_device,
        mesh=mesh,
        in_specs=(
            P(("worker", "expert"), None),
            P(("worker", "expert"), None),
            P(("worker", "expert"), None),
            P(("worker", "expert"), None),
            P("worker"),
            P(None, "expert"),
            P(None, "expert"),
            P("expert", None),
        ),
        out_specs=(
            P("worker", "expert"),
            P("worker", "expert"),
            P("expert", "worker"),
            P(("worker", "expert")),
        ),
        check_vma=False,
    )
```

profile of v0, /device:TPU:1, one launch (start us, length us, event | category | flops | bytes accessed | tf_op | source)
XLA Modules:
  0.0 847.8 jit_solution(9377517444615883189)
XLA Ops:
  14.1 7.3 gather_fusion
  23.4 185.0 %all_to_all.15 = bf16[16,80,3072]{2,1,0:T(8,128)(2,1)S(1)} all-to-all(bf16[16,80,3072]{2,1,0:T(8,128)(2,1)S(1)} %bitcast.48), channel_id=1, replica_groups=mesh['worker'=16,'expert'=16] {'expert'}, dimensions={0} | all-to-all | bytes 15728640 | tf_op jit(solution)/shard_map/all_to_all | solution.py:72
  211.6 3.5 multiply_convert_fusion.3
  215.1 5.3 convolution_convert_fusion
  220.4 6.8 all-to-all-start.1
  228.0 169.5 %all-to-all-done.1 = bf16[16,80,3072]{2,1,0:T(8,128)(2,1)} async-done(((bf16[16,80,3072]{2,1,0:T(8,128)(2,1)}), bf16[16,80,3072]{2,1,0:T(8,128)(2,1)}, u32[]{:S(2)}, u32[]{:S(2)}) %all-to-all-start.1) | async-done | bytes 7864352 | tf_op jit(solution)/shard_map/all_to_all | solution.py:77
  397.6 7.1 convert_reduce_fusion
  404.6 6.9 gather_fusion.1
  411.5 5.2 gather.21
  416.7 7.7 multiply_reduce_fusion
  424.8 2.8 mul.106
  427.7 5.2 mul.107
  435.2 3.4 gather_fusion.2
  440.4 4.1 broadcast_in_dim.78
  444.5 4.9 all-to-all-start.2
  450.3 162.8 %all-to-all-done.2 = bf16[16,80,3072]{2,1,0:T(8,128)(2,1)} async-done(((bf16[16,80,3072]{2,1,0:T(8,128)(2,1)}), bf16[16,80,3072]{2,1,0:T(8,128)(2,1)}, u32[]{:S(2)}, u32[]{:S(2)}) %all-to-all-start.2) | async-done | bytes 7864352 | tf_op jit(solution)/shard_map/all_to_all | solution.py:103
  613.1 7.6 fusion.2
  620.7 5.6 fusion.16
  627.4 6.9 fusion.1
  634.3 7.7 fusion
  642.0 48.7 %psum.7 = f32[]{:T(128)} all-reduce(f32[]{:T(128)} %bitcast), channel_id=1, replica_groups=mesh['worker'=16,'expert'=16] {'worker'}, use_global_device_ids=true, to_apply=%region_7.8 | all-reduce | flops 1 | bytes 8 | tf_op jit(solution)/shard_map/psum | solution.py:106
  691.3 14.0 %reduce-scatter.8.cloned.1.call-done = bf16[256,192]{0,1:T(8,128)(2,1)} async-done(((bf16[256,3072]{0,1:T(8,128)(2,1)}), bf16[256,192]{0,1:T(8,128)(2,1)}) %reduce-scatter.8.cloned.1.call-update) | async-done | bytes 98320 | tf_op jit(solution)/shard_map/reduce_scatter | solution.py:118
  707.5 64.6 %reduce-scatter.6.cloned.1.call-done = bf16[192,256]{1,0:T(8,128)(2,1)} async-done(((bf16[3072,256]{1,0:T(8,128)(2,1)}), bf16[192,256]{1,0:T(8,128)(2,1)}) %reduce-scatter.6.cloned.1.call-update) | async-done | bytes 98320 | tf_op jit(solution)/shard_map/reduce_scatter | solution.py:115
  774.2 64.6 %reduce-scatter.4.cloned.1.call-done = bf16[192,256]{1,0:T(8,128)(2,1)} async-done(((bf16[3072,256]{1,0:T(8,128)(2,1)}), bf16[192,256]{1,0:T(8,128)(2,1)}) %reduce-scatter.4.cloned.1.call-update) | async-done | bytes 98320 | tf_op jit(solution)/shard_map/reduce_scatter | solution.py:112
  (76 shorter events, 25.6 us)
Async XLA Ops:
  7.2 207.9 %copy-start = (bf16[256,3072]{1,0:T(8,128)(2,1)S(1)}, bf16[256,3072]{1,0:T(8,128)(2,1)}, u32[]{:S(2)}) copy-start(bf16[256,3072]{1,0:T(8,128)(2,1)} %param.15) | copy-start | bytes 4718596
  23.4 185.0 %copy-start.9 = (bf16[3072,256]{1,0:T(8,128)(2,1)S(1)}, bf16[3072,256]{1,0:T(8,128)(2,1)}, u32[]{:S(2)}) copy-start(bf16[3072,256]{1,0:T(8,128)(2,1)} %param.13) | copy-start | bytes 4718596
  208.4 3.2 copy-start.1
  208.4 3.2 copy-start.10
  211.6 3.5 copy-start.11
  215.1 5.3 copy-start.2
  220.4 7.1 copy-start.5
  220.4 7.2 copy-start.7
  220.4 7.5 copy-start.8
  220.4 177.1 %all-to-all-start.1 = ((bf16[16,80,3072]{2,1,0:T(8,128)(2,1)}), bf16[16,80,3072]{2,1,0:T(8,128)(2,1)}, u32[]{:S(2)}, u32[]{:S(2)}) async-start(bf16[16,80,3072]{2,1,0:T(8,128)(2,1)} %bitcast.46), calls=%async_computation.1 | async-start | bytes 15728640 | tf_op jit(solution)/shard_map/all_to_all | solution.py:77
  416.7 7.8 copy-start.4
  435.1 3.4 copy-start.6
  444.5 168.5 %copy-start.3 = (bf16[1280,256]{1,0:T(8,128)(2,1)S(1)}, bf16[1280,256]{1,0:T(8,128)(2,1)}, u32[]{:S(2)}) copy-start(bf16[1280,256]{1,0:T(8,128)(2,1)} %copy-done.2) | copy-start | bytes 1966084
  444.5 168.5 %all-to-all-start.2 = ((bf16[16,80,3072]{2,1,0:T(8,128)(2,1)}), bf16[16,80,3072]{2,1,0:T(8,128)(2,1)}, u32[]{:S(2)}, u32[]{:S(2)}) async-start(bf16[16,80,3072]{2,1,0:T(8,128)(2,1)} %bitcast.47), calls=%async_computation.2 | async-start | bytes 15728640 | tf_op jit(solution)/shard_map/all_to_all | solution.py:103
  449.4 255.9 %reduce-scatter.8.cloned.1.call-start = ((), (), s32[]{:S(2)}) async-start(), calls=%async_computation.8 | async-start | bytes 1671168 | tf_op jit(solution)/shard_map/reduce_scatter | solution.py:118
  620.7 6.7 copy-start.12
  620.7 151.4 %reduce-scatter.6.cloned.1.call-start = ((), (), s32[]{:S(2)}) async-start(), calls=%async_computation.7 | async-start | bytes 1671168 | tf_op jit(solution)/shard_map/reduce_scatter | solution.py:115
  626.3 1.1 copy-start.13
  634.3 204.6 %reduce-scatter.4.cloned.1.call-start = ((), (), s32[]{:S(2)}) async-start(), calls=%async_computation.6 | async-start | bytes 1671168 | tf_op jit(solution)/shard_map/reduce_scatter | solution.py:112
Sparse Core Ops, SparseCore 0:
  620.8 84.4 reduce-scatter.7
  707.8 64.1 reduce-scatter.5
  774.6 64.2 reduce-scatter.3
where the time goes:
time: 855 us; the launch traced here: 848 us
  waiting for transfers between devices  476 us (56%)
  blocking collectives  234 us (27%)
  local copies, waits for them, and re-layouts  42.9 us (5%)
  matrix products  38.8 us (5%)
  other arithmetic  29.8 us (3%)
  between operations  14.9 us (2%)
  starting transfers between devices  12 us (1%)
    all_to_all x1, blocking collectives, per_device(): lax.all_to_all(send_tokens, 'expert', split_axis=0, concat_axis=0, tiled=...  185 us
    all_to_all x1, waiting for transfers between devices, per_device(): lax.all_to_all(partial_slots.reshape(expert_devices, CAP, width), 'expert...  170 us
    all_to_all x1, waiting for transfers between devices, per_device(): lax.all_to_all(send_cot, 'expert', split_axis=0, concat_axis=0, tiled=True)  163 us
    reduce_scatter x1, waiting for transfers between devices, per_device(): lax.psum_scatter((weight * gate_grad).astype(jnp.bfloat16), 'worker', sca...  64.6 us
    reduce_scatter x1, waiting for transfers between devices, per_device(): lax.psum_scatter((weight * up_grad).astype(jnp.bfloat16), 'worker', scatt...  64.6 us
    psum x1, blocking collectives, per_device(): total_steps = lax.psum(weight, 'worker')  48.7 us
    dot_general x3, matrix products, contract_rows(): lax.dot_general(left, right, (((0,), (0,)), ((), ())), preferred_element_...  22.2 us
  transfers between devices with their start and end apart: 5, of which 5 were waited for; matrix products, arithmetic and copies ran while one was open for 3% of the time, Pallas kernels for 0%

commit v1 on v0

v1 whole, which is shorter than its diff:
```python
import functools

import jax
import jax.numpy as jnp
from jax import lax
from jax.experimental import pallas as pl
from jax.experimental.pallas import tpu as pltpu
from jax.sharding import PartitionSpec as P

MESH = pl.DeviceIdType.MESH
F32 = jnp.float32
BF16 = jnp.bfloat16
EXPERTS = 4
TOK = 128
D = 3072
HALF = TOK // 2
DC = 768
DB = 384


class Ids:
    def __init__(self):
        self.n = 0

    def take(self, count):
        base = self.n
        self.n += count
        return base


IDS = Ids()
T_RA, T_RB, T_LA, T_LB, T_FR, T_FL, T_C, T_CL, T_CR, T_CF = (IDS.take(1) for _ in range(10))
MT = IDS.take(8)
ST = IDS.take(16)
Z1, Z2, Z3, Z4 = (IDS.take(6) for _ in range(4))
YQ = IDS.take(24)
PX = IDS.take(4)
RX = IDS.take(24)
AG = IDS.take(40)
ZR = IDS.take(72)
YB = IDS.take(6)
YS = IDS.take(12)
FX = IDS.take(3)
N_SEM = IDS.n


def kernel(
    meta, tok, tgt, gw, uw, dw, out, loss,
    X, W1, WD, GU, H, HS, MXB, META, STEPS, R, PSD, PRV, XR, TG, G, GG, DM, ZH, ZF,
    YR1, YR2, FS, FR, LS, ssem, rsem, lsem,
):
    w = lax.axis_index("worker")
    ex = lax.axis_index("expert")
    y, zl, c = w // 4, (w // 2) % 2, w % 2
    p, x = ex // 4, ex % 4
    z = p * 2 + zl
    oc = 1 - c
    oz = 1 - zl
    xr, xl, x2 = (x + 1) % 4, (x + 3) % 4, (x + 2) % 4
    yu, yd, y2 = (y + 1) % 4, (y + 3) % 4, (y + 2) % 4
    e_out, e_in, e_opp = (p + 2 * zl + 3) % 4, (p + 5 - 2 * zl) % 4, (p + 2) % 4
    own = c * 4 + x
    right = (w, p * 4 + xr)
    left = (w, p * 4 + xl)
    core = (y * 4 + zl * 2 + oc, ex)
    z_out = (y * 4 + oz * 2 + c, e_out * 4 + x)
    z_in = (y * 4 + oz * 2 + c, ex)
    y_up = (yu * 4 + zl * 2 + c, ex)
    y_dn = (yd * 4 + zl * 2 + c, ex)
    zu, zd = (z + 1) % 8, (z + 7) % 8
    z_up = (y * 4 + (zu % 2) * 2 + c, (zu // 2) * 4 + x)
    z_dn = (y * 4 + (zd % 2) * 2 + c, (zd // 2) * 4 + x)

    def rc(i, src, dst, dev):
        return pltpu.make_async_remote_copy(
            src_ref=src, dst_ref=dst, send_sem=ssem.at[i], recv_sem=rsem.at[i],
            device_id=dev, device_id_type=MESH,
        )

    pending = []

    def send(i, src, dst, dev):
        copy = rc(i, src, dst, dev)
        copy.start()
        pending.append(copy)

    def send_later(i, src, dst, dev):
        rc(i, src, dst, dev).start()

    def arrived(i, dst):
        rc(i, dst, dst, core).wait_recv()

    def drain():
        for copy in pending:
            copy.wait_send()
        pending.clear()

    barrier = pltpu.get_barrier_semaphore()

    def greet(dev):
        pl.semaphore_signal(barrier, inc=1, device_id=dev, device_id_type=MESH)

    def slot_dev(s):
        return (y * 4 + zl * 2 + s // 4, p * 4 + s % 4)

    for i in range(1, 8):
        greet(slot_dev((own + i) % 8))
    for i in range(1, 16):
        other = (w + i) % 16
        greet((other, ex))
    greet(z_out)
    pl.semaphore_wait(barrier, 23)

    loads = [
        pltpu.make_async_copy(gw.at[:, pl.ds(c * 128, 128)], W1.at[p, 0], lsem.at[0]),
        pltpu.make_async_copy(uw.at[:, pl.ds(c * 128, 128)], W1.at[p, 1], lsem.at[1]),
        pltpu.make_async_copy(dw.at[pl.ds(c * 128, 128)], WD.at[p], lsem.at[2]),
        pltpu.make_async_copy(tok, X.at[own], lsem.at[3]),
        pltpu.make_async_copy(tgt, TG, lsem.at[4]),
        pltpu.make_async_copy(meta, META.at[own], lsem.at[5]),
        pltpu.make_async_copy(meta, STEPS.at[w], lsem.at[6]),
    ]
    for load in (loads[1], loads[2], loads[0]):
        load.start()

    A, B = pl.ds(0, HALF), pl.ds(HALF, HALF)
    send(T_RA, tok.at[A], X.at[own, A], right)
    send(T_LB, tok.at[B], X.at[own, B], left)
    send(T_RB, tok.at[B], X.at[own, B], right)
    send(T_LA, tok.at[A], X.at[own, A], left)
    send(T_C, tok, X.at[own], core)
    for load in loads[3:]:
        load.start()

    def chunk(e, k, q):
        if k == 1:
            return WD.at[e, pl.ds(32 * q, 32)]
        return W1.at[e, 1 if k == 0 else 0, pl.ds(768 * q, 768)]

    def zchunk(e, k):
        return chunk(e, k, y if k < 2 else k - 2)

    def half(e, k, q, h):
        if k == 1:
            return WD.at[e, pl.ds(32 * q + 16 * h, 16)]
        return W1.at[e, 1 if k == 0 else 0, pl.ds(768 * q + 384 * h, 384)]

    def zhalf(e, k, h):
        return half(e, k, y if k < 2 else k - 2, h)

    def z1(k):
        send(Z1 + k, zchunk(p, k), zchunk(p, k), z_out)

    def z2(k):
        arrived(Z1 + k, zchunk(e_out, k))
        send(Z2 + k, zchunk(e_out, k), zchunk(e_out, k), z_in)

    def z3(k):
        arrived(Z2 + k, zchunk(e_in, k))
        send(Z3 + k, zhalf(e_in, k, oz), zhalf(e_in, k, oz), z_out)

    def z4(k):
        arrived(Z3 + k, zhalf(e_opp, k, zl))
        send(Z4 + k, zhalf(e_opp, k, zl), zhalf(e_opp, k, zl), z_in)

    def z5(k):
        arrived(Z4 + k, zhalf(e_opp, k, oz))

    es = (e_out, e_in, e_opp)

    def yq(n, k):
        i = YQ + (n * 2 + k) * 4
        send(i, chunk(es[n], k, y), chunk(es[n], k, y), y_up)
        send(i + 1, chunk(es[n], k, y), chunk(es[n], k, y), y_dn)

    def yf(n, k):
        i = YQ + (n * 2 + k) * 4
        arrived(i, chunk(es[n], k, yd))
        send(i + 2, half(es[n], k, yd, 0), half(es[n], k, yd, 0), y_up)
        arrived(i + 1, chunk(es[n], k, yu))
        send(i + 3, half(es[n], k, yu, 1), half(es[n], k, yu, 1), y_dn)

    def ye(n, k):
        i = YQ + (n * 2 + k) * 4
        arrived(i + 2, half(es[n], k, y2, 0))
        arrived(i + 3, half(es[n], k, y2, 1))

    loads[1].wait()
    z1(0)
    loads[2].wait()
    z1(1)
    loads[0].wait()
    z1(2)

    @pl.loop(1, 8)
    def _(i):
        send_later(MT + i, meta, META.at[own], slot_dev((own + i) % 8))

    @pl.loop(1, 16)
    def _(i):
        send_later(ST + i, meta, STEPS.at[w], ((w + i) % 16, ex))

    z2(0)
    yq(0, 0)
    arrived(T_RA, X.at[c * 4 + xl, A])
    send(T_FR, X.at[c * 4 + xl, A], X.at[c * 4 + xl, A], right)
    arrived(T_LB, X.at[c * 4 + xr, B])
    send(T_FL, X.at[c * 4 + xr, B], X.at[c * 4 + xr, B], left)
    z2(1)
    yq(0, 1)
    z3(0)
    yq(1, 0)
    z1(3)
    yf(0, 0)
    z2(2)
    z3(1)
    yq(1, 1)
    z1(4)
    arrived(T_RB, X.at[c * 4 + xl, B])
    send(T_CL, X.at[c * 4 + xl], X.at[c * 4 + xl], core)
    arrived(T_LA, X.at[c * 4 + xr, A])
    send(T_CR, X.at[c * 4 + xr], X.at[c * 4 + xr], core)
    z4(0)
    z3(2)
    z1(5)
    z2(3)
    z5(0)
    yq(2, 0)
    yf(0, 1)
    yf(1, 0)
    z4(1)
    z5(1)
    yq(2, 1)
    arrived(T_FR, X.at[c * 4 + x2, A])
    arrived(T_FL, X.at[c * 4 + x2, B])
    send(T_CF, X.at[c * 4 + x2], X.at[c * 4 + x2], core)
    yf(1, 1)
    z2(4)
    z3(3)
    z4(2)
    z2(5)
    yf(2, 0)
    z3(4)
    z4(3)
    yf(2, 1)
    z3(5)
    z4(4)
    z4(5)

    for load in loads[3:]:
        load.wait()

    @pl.loop(1, 8)
    def _(i):
        arrived(MT + i, META.at[(own + 8 - i) % 8])

    @pl.loop(1, 16)
    def _(i):
        arrived(ST + i, STEPS.at[(w + 16 - i) % 16])

    lane = lax.broadcasted_iota(jnp.int32, (TOK, 128), 1)
    eye = lane == lax.broadcasted_iota(jnp.int32, (TOK, 128), 0)

    @pl.loop(0, 8)
    def _(s):
        rows = META[s]
        cols = jnp.zeros((TOK, 128), F32)
        for r in range(5):
            spread = jnp.where(eye, jnp.broadcast_to(rows[r : r + 1, :], (TOK, 128)), 0.0)
            cols = cols + jnp.where(lane == r, jnp.sum(spread, axis=1, keepdims=True), 0.0)
        MXB[s] = cols

    arrived(T_C, X.at[oc * 4 + x])
    arrived(T_CL, X.at[oc * 4 + xl])
    arrived(T_CR, X.at[oc * 4 + xr])
    arrived(T_CF, X.at[oc * 4 + x2])
    for k in range(2, 6):
        z5(k)
    for n in range(3):
        for k in range(2):
            ye(n, k)

    lane4 = lax.broadcasted_iota(jnp.int32, (512, 128), 1)

    def column(mb, r):
        rows = MXB[pl.ds(4 * mb, 4)].reshape(512, 128)
        return jnp.sum(jnp.where(lane4 == r, rows, 0.0), axis=1, keepdims=True)

    @pl.loop(0, 8)
    def _(i):
        e, mb = i // 2, i % 2
        rows = X[pl.ds(4 * mb, 4)].reshape(512, D)
        weights = jnp.concatenate([W1[e, 0], W1[e, 1]], axis=1)
        pre = jnp.dot(rows, weights, preferred_element_type=F32)
        GU[e, mb] = pre
        gate, up = pre[:, :128], pre[:, 128:]
        mixed = gate * jax.nn.sigmoid(gate) * up * column(mb, e)
        at = (pl.ds(pl.multiple_of(512 * mb, 512), 512), pl.ds(pl.multiple_of(128 * e, 128), 128))
        H[at] = mixed.astype(BF16)
        HS[at] = (mixed * column(mb, 4)).astype(BF16)

    drain()

    @pl.loop(1, 8)
    def _(i):
        rc(MT + i, meta, META.at[own], core).wait_send()

    @pl.loop(1, 16)
    def _(i):
        rc(ST + i, meta, STEPS.at[w], core).wait_send()

    G[...] = jnp.zeros_like(G)
    LS[...] = jnp.zeros_like(LS)

    def dcols(j):
        return pl.ds(pl.multiple_of(DC * j, DC), DC)

    def wd_cols(j):
        return WD[:, :, dcols(j)].reshape(512, DC)

    def hrows(who):
        return H[pl.ds(pl.multiple_of(512 * who, 512), 512), :]

    def s0(j):
        slot = j % 2

        @pl.when(j >= 2)
        def _():
            rc(PX + j - 2, PSD.at[slot], PRV.at[j - 2], core).wait_send()

        part = jnp.dot(hrows(oc), wd_cols(j), preferred_element_type=F32)
        PSD[slot] = part.astype(BF16).reshape(4, TOK, DC)
        send_later(PX + j, PSD.at[slot], PRV.at[j], core)

    def rs_copy(j, n):
        src = (
            PRV.at[j, x2, A], PRV.at[j, x2, B], PRV.at[j, xr, B], PRV.at[j, xl, A],
            PRV.at[j, xr, A], PRV.at[j, xl, B],
        )[n]
        return rc(RX + 6 * j + n, src, XR.at[j, n], right if n % 2 == 0 else left)

    def s1(j):
        arrived(PX + j, PRV.at[j])
        part = jnp.dot(hrows(c), wd_cols(j), preferred_element_type=F32)
        both = part.reshape(4, TOK, DC) + PRV[j].astype(F32)
        PRV[j] = both.astype(BF16)
        for n in range(4):
            rs_copy(j, n).start()

    def add_into(ref, other):
        ref[...] = (ref[...].astype(F32) + other[...].astype(F32)).astype(BF16)

    def s2(j):
        arrived(RX + 6 * j, XR.at[j, 0])
        add_into(PRV.at[j, xr, A], XR.at[j, 0])
        rs_copy(j, 4).start()
        arrived(RX + 6 * j + 1, XR.at[j, 1])
        add_into(PRV.at[j, xl, B], XR.at[j, 1])
        rs_copy(j, 5).start()

    def ag_copy(j, n):
        i = AG + 10 * j + n
        if n < 4:
            h = (A, B, B, A)[n]
            return rc(i, R.at[j, own, h], R.at[j, own, h], (right, left)[n % 2])
        if n == 4:
            return rc(i, R.at[j, own], R.at[j, own], core)
        if n == 5:
            return rc(i, R.at[j, c * 4 + xl, A], R.at[j, c * 4 + xl, A], right)
        if n == 6:
            return rc(i, R.at[j, c * 4 + xr, B], R.at[j, c * 4 + xr, B], left)
        s = c * 4 + (xl, xr, x2)[n - 7]
        return rc(i, R.at[j, s], R.at[j, s], core)

    def ag_arrived(j, n):
        i = AG + 10 * j + n
        near = c * 4 + (xl if n in (0, 2) else xr)
        far = oc * 4
        dst = {
            0: R.at[j, near, A], 2: R.at[j, near, B], 1: R.at[j, near, B], 3: R.at[j, near, A],
            4: R.at[j, far + x], 5: R.at[j, c * 4 + x2, A], 6: R.at[j, c * 4 + x2, B],
            7: R.at[j, far + xl], 8: R.at[j, far + xr], 9: R.at[j, far + x2],
        }[n]
        arrived(i, dst)

    def s3(j):
        for n in (2, 3, 4, 5):
            arrived(RX + 6 * j + n, XR.at[j, n])
        base = PRV[j, x].astype(F32)
        top = base[:HALF] + XR[j, 4].astype(F32) + XR[j, 3].astype(F32)
        low = base[HALF:] + XR[j, 2].astype(F32) + XR[j, 5].astype(F32)
        mixed = jnp.concatenate([top, low], axis=0)
        resid = mixed - TG[:, dcols(j)].astype(F32)
        square = resid * resid
        folded = square[:, :128]
        for n in range(1, 6):
            folded = folded + square[:, 128 * n : 128 * (n + 1)]
        LS[...] += folded
        R[j, own] = resid.astype(BF16)
        for n in (0, 1, 2, 3, 4):
            ag_copy(j, n).start()

    def s4(j):
        ag_arrived(j, 0)
        ag_copy(j, 5).start()
        ag_arrived(j, 1)
        ag_copy(j, 6).start()
        ag_arrived(j, 2)
        ag_copy(j, 7).start()
        ag_arrived(j, 3)
        ag_copy(j, 8).start()

    def s5(j):
        ag_arrived(j, 5)
        ag_arrived(j, 6)
        ag_copy(j, 9).start()

    def piece(m, j, dest):
        return DM.at[m, dest // 2, j, dest % 2]

    def z_copy(q, m, j, step, way):
        i = ZR + 8 * q + 2 * step + way
        dest = (z + (4 - step if way == 0 else 4 + step)) % 8
        dev = z_up if way == 0 else z_dn
        if step == 0:
            return rc(i, piece(m, j, dest).at[A if way == 0 else B], ZH.at[q, way], dev)
        return rc(i, piece(m, j, dest), ZF.at[q, way, step - 1], dev)

    def z_start(q, m, j):
        z_copy(q, m, j, 0, 0).start()
        z_copy(q, m, j, 0, 1).start()

    def z_step(q, m, j, step):
        for way in range(2):
            i = ZR + 8 * q + 2 * (step - 1) + way
            dest = (z + (4 - step if way == 0 else 4 + step)) % 8
            if step == 1:
                arrived(i, ZH.at[q, way])
                add_into(piece(m, j, dest).at[A if way == 0 else B], ZH.at[q, way])
            else:
                arrived(i, ZF.at[q, way, step - 2])
                add_into(piece(m, j, dest), ZF.at[q, way, step - 2])
            z_copy(q, m, j, step, way).start()

    def z_sum(q, m, j):
        for way in range(2):
            arrived(ZR + 8 * q + 6 + way, ZF.at[q, way, 2])
        mine = piece(m, j, z)[...].astype(F32)
        return mine + ZF[q, 0, 2].astype(F32) + ZF[q, 1, 2].astype(F32)

    def z_end(q, m, j):
        total = z_sum(q, m, j)
        DM[m, p, j, zl] = total.astype(BF16)

    def z_drain(q, m, j):
        for step in range(4):
            for way in range(2):
                z_copy(q, m, j, step, way).wait_send()

    def s6(j):
        for n in (4, 7, 8, 9):
            ag_arrived(j, n)
        rows = R[j].reshape(1024, DC)
        down = lax.dot_general(HS[...], rows, (((0,), (0,)), ((), ())), preferred_element_type=F32)
        for e in range(4):
            for b in range(2):
                DM[2, e, j, b] = down[128 * e : 128 * (e + 1), DB * b : DB * (b + 1)].astype(BF16)
        z_start(j, 2, j)
        G[...] += lax.dot_general(
            rows, wd_cols(j), (((1,), (1,)), ((), ())), preferred_element_type=F32
        )

    stages = [s1, s2, s3, s4, s5, s6] + [
        functools.partial(lambda j, step: z_step(j, 2, j, step), step=step) for step in (1, 2, 3)
    ]

    @pl.loop(0, 10)
    def _(t):
        @pl.when(t < 4)
        def _():
            s0(t)

        for n, stage in enumerate(stages):
            j = t - (n + 1)

            @pl.when((j >= 0) & (j < 4))
            def _():
                stage(j)

    mean = jnp.sum(LS[...], axis=1, keepdims=True) * (0.5 / D)
    loss[...] = jnp.sum(jnp.where(eye, mean, 0.0), axis=0, keepdims=True)

    @pl.loop(0, 8)
    def _(i):
        e, mb = i // 2, i % 2
        at = (pl.ds(pl.multiple_of(512 * mb, 512), 512), pl.ds(pl.multiple_of(128 * e, 128), 128))
        grad = G[at] * (column(mb, e) * column(mb, 4))
        pre = GU[e, mb]
        gate, up = pre[:, :128], pre[:, 128:]
        sig = jax.nn.sigmoid(gate)
        rows = at[0]
        GG[rows, pl.ds(pl.multiple_of(256 * e, 128), 128)] = (
            grad * up * (sig * (1.0 + gate * (1.0 - sig)))
        ).astype(BF16)
        GG[rows, pl.ds(pl.multiple_of(256 * e + 128, 128), 128)] = (grad * (gate * sig)).astype(BF16)

    def dw_chunk(j):
        rows = X[:, :, dcols(j)].reshape(1024, DC)

        @pl.loop(0, 4)
        def _(e):
            left_rows = GG[:, pl.ds(pl.multiple_of(256 * e, 256), 256)]
            grads = lax.dot_general(left_rows, rows, (((0,), (0,)), ((), ())), preferred_element_type=F32)
            for m in range(2):
                for b in range(2):
                    DM[m, e, j, b] = grads[128 * m : 128 * (m + 1), DB * b : DB * (b + 1)].astype(BF16)

    lo, hi = pl.ds(0, 2), pl.ds(2, 2)

    def yb_copy(n):
        src = (
            DM.at[0, lo, y2], DM.at[0, hi, y2], DM.at[0, hi, yu], DM.at[0, lo, yd],
            DM.at[0, lo, yu], DM.at[0, hi, yd],
        )[n]
        return rc(YB + n, src, YR1.at[n], y_up if n % 2 == 0 else y_dn)

    def ys_copy(m, n):
        src = (
            DM.at[m, p, y2, zl, A], DM.at[m, p, y2, zl, B], DM.at[m, p, yu, zl, B],
            DM.at[m, p, yd, zl, A], DM.at[m, p, yu, zl, A], DM.at[m, p, yd, zl, B],
        )[n]
        return rc(YS + 6 * (m - 1) + n, src, YR2.at[m - 1, n], y_up if n % 2 == 0 else y_dn)

    def yb_add(n, ref):
        arrived(YB + n, YR1.at[n])
        for a in range(2):
            for b in range(2):
                add_into(ref.at[a, b], YR1.at[n, a, b])

    def ys_start(m):
        for n in range(4):
            ys_copy(m, n).start()

    def ys_step(m):
        arrived(YS + 6 * (m - 1), YR2.at[m - 1, 0])
        add_into(DM.at[m, p, yu, zl, A], YR2.at[m - 1, 0])
        ys_copy(m, 4).start()
        arrived(YS + 6 * (m - 1) + 1, YR2.at[m - 1, 1])
        add_into(DM.at[m, p, yd, zl, B], YR2.at[m - 1, 1])
        ys_copy(m, 5).start()

    def ys_sum(m):
        for n in range(2, 6):
            arrived(YS + 6 * (m - 1) + n, YR2.at[m - 1, n])
        mine = DM[m, p, y, zl].astype(F32)
        top = mine[:HALF] + YR2[m - 1, 4].astype(F32) + YR2[m - 1, 3].astype(F32)
        low = mine[HALF:] + YR2[m - 1, 2].astype(F32) + YR2[m - 1, 5].astype(F32)
        return jnp.concatenate([top, low], axis=0)

    total_steps = jnp.sum(STEPS[...], axis=0)[4:5, :]
    mine_rows = pl.ds(pl.multiple_of(192 * c, 192), 192)
    other_rows = pl.ds(pl.multiple_of(192 * oc, 192), 192)

    def finish(m, total):
        FS[m] = total.T / total_steps
        rc(FX + m, FS.at[m, other_rows], FR.at[m], core).start()

    def up_step(n, step):
        j = (y2, yu, yd, y)[n]
        if step == 0:
            z_start(4 + n, 1, j)
        elif step < 4:
            z_step(4 + n, 1, j, step)
        else:
            z_end(4 + n, 1, j)

    z_step(1, 2, 1, 3)
    z_step(2, 2, 2, 2)
    z_step(3, 2, 3, 1)
    dw_chunk(y2)
    yb_copy(0).start()
    yb_copy(1).start()
    up_step(0, 0)
    z_end(0, 2, 0)
    z_step(2, 2, 2, 3)
    z_step(3, 2, 3, 2)
    dw_chunk(yu)
    yb_copy(2).start()
    up_step(1, 0)
    z_end(1, 2, 1)
    z_step(3, 2, 3, 3)
    dw_chunk(yd)
    yb_copy(3).start()
    up_step(2, 0)
    up_step(0, 1)
    dw_chunk(y)
    up_step(3, 0)
    yb_add(0, DM.at[0, lo, yu])
    yb_copy(4).start()
    yb_add(1, DM.at[0, hi, yd])
    yb_copy(5).start()
    z_end(2, 2, 2)
    z_end(3, 2, 3)
    ys_start(2)
    up_step(1, 1)
    up_step(0, 2)
    up_step(2, 1)
    up_step(1, 2)
    up_step(0, 3)
    up_step(3, 1)
    ys_step(2)
    up_step(2, 2)
    up_step(1, 3)
    up_step(0, 4)
    up_step(3, 2)
    up_step(2, 3)
    up_step(1, 4)
    up_step(3, 3)
    finish(2, ys_sum(2))
    yb_add(3, DM.at[0, lo, y])
    yb_add(4, DM.at[0, lo, y])
    yb_add(2, DM.at[0, hi, y])
    yb_add(5, DM.at[0, hi, y])
    z_start(8, 0, y)
    up_step(2, 4)
    up_step(3, 4)
    ys_start(1)
    z_step(8, 0, y, 1)
    ys_step(1)
    z_step(8, 0, y, 2)
    finish(1, ys_sum(1))
    z_step(8, 0, y, 3)
    finish(0, z_sum(8, 0, y))

    lanes = pl.ds(pl.multiple_of(128 * c, 128), 128)
    other_lanes = pl.ds(pl.multiple_of(128 * oc, 128), 128)
    for m in (2, 1, 0):
        out[m, :, lanes] = FS[m, mine_rows]
        arrived(FX + m, FR.at[m])
        out[m, :, other_lanes] = FR[m]

    @pl.loop(0, 4)
    def _(j):
        @pl.when(j >= 2)
        def _():
            rc(PX + j, PSD.at[j % 2], PRV.at[j], core).wait_send()

        for n in range(6):
            rs_copy(j, n).wait_send()
        for n in range(10):
            ag_copy(j, n).wait_send()
        z_drain(j, 2, j)

    for n in range(4):
        z_drain(4 + n, 1, (y2, yu, yd, y)[n])
    z_drain(8, 0, y)
    for n in range(6):
        yb_copy(n).wait_send()
        ys_copy(1, n).wait_send()
        ys_copy(2, n).wait_send()
    for m in range(3):
        rc(FX + m, FS.at[m, other_rows], FR.at[m], core).wait_send()


def per_device(tokens, route_ids, route_mix, target, step_count, gate_weight, up_weight, down_weight):
    experts = jnp.arange(EXPERTS, dtype=jnp.int32)[:, None, None]
    mix = jnp.sum(jnp.where(route_ids[None] == experts, route_mix[None], 0.0), axis=2)
    step = jnp.broadcast_to(step_count.astype(F32)[:, None], (1, TOK))
    meta = jnp.concatenate([mix, step, jnp.zeros((3, TOK), F32)], axis=0)
    any_spec = pl.BlockSpec(memory_space=pl.ANY)
    vmem_spec = pl.BlockSpec(memory_space=pltpu.VMEM)
    out, loss = pl.pallas_call(
        kernel,
        out_shape=(
            jax.ShapeDtypeStruct((3, 192, 256), F32),
            jax.ShapeDtypeStruct((1, TOK), F32),
        ),
        in_specs=[any_spec] * 6,
        out_specs=(vmem_spec, vmem_spec),
        scratch_shapes=[
            pltpu.VMEM((8, TOK, D), BF16),
            pltpu.VMEM((4, 2, D, 128), BF16),
            pltpu.VMEM((4, 128, D), BF16),
            pltpu.VMEM((4, 2, 512, 256), F32),
            pltpu.VMEM((1024, 512), BF16),
            pltpu.VMEM((1024, 512), BF16),
            pltpu.VMEM((8, TOK, 128), F32),
            pltpu.VMEM((8, 8, 128), F32),
            pltpu.VMEM((16, 8, 128), F32),
            pltpu.VMEM((4, 8, TOK, DC), BF16),
            pltpu.VMEM((2, 4, TOK, DC), BF16),
            pltpu.VMEM((4, 4, TOK, DC), BF16),
            pltpu.VMEM((4, 6, HALF, DC), BF16),
            pltpu.VMEM((TOK, D), BF16),
            pltpu.VMEM((1024, 512), F32),
            pltpu.VMEM((1024, 1024), BF16),
            pltpu.VMEM((3, 4, 4, 2, 128, DB), BF16),
            pltpu.VMEM((9, 2, HALF, DB), BF16),
            pltpu.VMEM((9, 2, 3, 128, DB), BF16),
            pltpu.VMEM((6, 2, 2, 128, DB), BF16),
            pltpu.VMEM((2, 6, HALF, DB), BF16),
            pltpu.VMEM((3, DB, 128), F32),
            pltpu.VMEM((3, 192, 128), F32),
            pltpu.VMEM((TOK, 128), F32),
            pltpu.SemaphoreType.DMA((N_SEM,)),
            pltpu.SemaphoreType.DMA((N_SEM,)),
            pltpu.SemaphoreType.DMA((7,)),
        ],
        compiler_params=pltpu.CompilerParams(
            collective_id=0, has_side_effects=True, vmem_limit_bytes=67043328
        ),
    )(meta, tokens, target, gate_weight, up_weight, down_weight)
    return out[0], out[1], out[2].T, loss.reshape(TOK)


def solution(mesh):
    return jax.shard_map(
        per_device,
        mesh=mesh,
        in_specs=(
            P(("worker", "expert"), None),
            P(("worker", "expert"), None),
            P(("worker", "expert"), None),
            P(("worker", "expert"), None),
            P("worker"),
            P(None, "expert"),
            P(None, "expert"),
            P("expert", None),
        ),
        out_specs=(
            P("worker", "expert"),
            P("worker", "expert"),
            P("expert", "worker"),
            P(("worker", "expert")),
        ),
        check_vma=False,
    )
```

time: 855 us -> 216 us (0.25)
  waiting for transfers between devices: 476 us -> 0 us
  blocking collectives: 234 us -> 0 us
  Pallas kernels: 0 us -> 210 us
  local copies, waits for them, and re-layouts: 42.9 us -> 3.19 us
  matrix products: 38.8 us -> 0 us
  other arithmetic: 29.8 us -> 1.37 us
  between operations: 14.9 us -> 1.29 us
  starting transfers between devices: 12 us -> 0 us
    all_to_all x2 -> x0, waiting for transfers between devices: 332 us -> none  [the longest x1 170 us: per_device(): lax.all_to_all(partial_slots.reshape(expert_devices, CAP, width), 'expert...]
    pallas_call x0 -> x1, Pallas kernels: none -> 210 us  [per_device(): pl.pallas_call(kernel, out_shape=(jax.ShapeDtypeStruct((3, 192, 256), F32...]
    all_to_all x1 -> x0, blocking collectives: 185 us -> none  [per_device(): lax.all_to_all(send_tokens, 'expert', split_axis=0, concat_axis=0, tiled=...]
    reduce_scatter x3 -> x0, waiting for transfers between devices: 143 us -> none  [the longest x1 64.6 us: per_device(): lax.psum_scatter((weight * gate_grad).astype(jnp.bfloat16), 'worker', sca...]
    psum x1 -> x0, blocking collectives: 48.7 us -> none  [per_device(): total_steps = lax.psum(weight, 'worker')]
    dot_general x7 -> x0, matrix products: 38.8 us -> none  [the longest x3 22.2 us: contract_rows(): lax.dot_general(left, right, (((0,), (0,)), ((), ())), preferred_element_...]
    gather x4 -> x0, local copies, waits for them, and re-layouts: 22.8 us -> none  [the longest x2 12.1 us: per_device(): jnp.take(expert_out, slot_key, axis=0).reshape(tok_dev, topk, width)]
    reduce_sum x4 -> x1, other arithmetic: 15.2 us -> 0.71 us  [per_device(): jnp.sum(jnp.where(route_ids[None] == experts, route_mix[None], 0.0), axis=2)]
  transfers between devices with their start and end apart: 5 -> 0, of which waited for: 5 -> 0; matrix products, arithmetic and copies ran while one was open for 3% -> 0% of each run, Pallas kernels for 0% -> 0%
where the time goes in v1:
time: 216 us
  Pallas kernels  210 us (97%)
  local copies, waits for them, and re-layouts  3.19 us (1%)
    pallas_call x1, Pallas kernels, per_device(): pl.pallas_call(kernel, out_shape=(jax.ShapeDtypeStruct((3, 192, 256), F32...  210 us

profile of v1, /device:TPU:1, one launch (start us, length us, event | category | flops | bytes accessed | tf_op | source)
XLA Modules:
  0.0 216.2 jit_solution(3964350866029719452)
XLA Ops:
  1.3 0.1 pad.1.clone
  1.4 0.1 pad.2.clone
  1.4 0.7 select_reduce_fusion
  2.1 0.7 maximum_maximum_fusion.meta
  2.8 210.4 %shard_map.111 = (f32[3,192,256]{2,1,0:T(8,128)}, f32[1,128]{1,0:T(1,128)}) custom-call(f32[8,128]{1,0:T(8,128)} %maximum_maximum_fusion.meta, bf16[128,3072]{1,0:T(8,128)(2,1)} %tok.1, bf16[128,3072]{1,0:T(8,128)(2,1)} %tgt.1, bf16[3072,256]{1,0:T(8,128)(2,1)} %gw.1, bf16[3072,256]{1,0:T(8,128)(2,1)} %uw.1, bf16[256,3072]{1,0:T(8,128)(2,1)} %dw.1), custom_call_target="tpu_custom_call" | custom-call | tf_op jit(solution)/shard_map/pallas_call | solution.py:672
  213.2 1.9 slice_bitcast_fusion
  215.1 1.1 copy.16
  (1 shorter events, 0.0 us)

commit v2 on v1

v2 whole, which is shorter than its diff:
```python
import functools

import jax
import jax.numpy as jnp
from jax import lax
from jax.experimental import pallas as pl
from jax.experimental.pallas import tpu as pltpu
from jax.sharding import PartitionSpec as P

MESH = pl.DeviceIdType.MESH
F32 = jnp.float32
BF16 = jnp.bfloat16
EXPERTS = 4
TOK = 128
D = 3072
HALF = TOK // 2
DC = 768
DB = 384


class Ids:
    def __init__(self):
        self.n = 0

    def take(self, count):
        base = self.n
        self.n += count
        return base


IDS = Ids()
T_RA, T_RB, T_LA, T_LB, T_FR, T_FL, T_C, T_CL, T_CR, T_CF = (IDS.take(1) for _ in range(10))
MS = IDS.take(1)
Z1, Z2, Z3, Z4 = (IDS.take(9) for _ in range(4))
YQ = IDS.take(36)
PX = IDS.take(4)
RX = IDS.take(24)
AG = IDS.take(40)
ZR = IDS.take(72)
YB = IDS.take(6)
YS = IDS.take(6)
FX = IDS.take(3)
N_SEM = IDS.n
S_TOK, S_W, S_META, S_RX, S_AG, S_YB, S_YS, S_PX, S_ZR, N_SEND = 0, 1, 2, 3, 4, 5, 6, 8, 12, 21
S_FX = N_SEND
N_SEND += 3


def kernel(
    meta, tok, tgt, gw, uw, dw, out,
    X, W1, WD, GU, H, HS, MXB, META, STEPS, R, PSD, PRV, XR, TG, G, GG, DM, ZH, ZF,
    YR1, YR2, FS, FR, LS, ssem, rsem, lsem,
):
    w = lax.axis_index("worker")
    ex = lax.axis_index("expert")
    y, zl, c = w // 4, (w // 2) % 2, w % 2
    p, x = ex // 4, ex % 4
    z = p * 2 + zl
    oc = 1 - c
    oz = 1 - zl
    xr, xl, x2 = (x + 1) % 4, (x + 3) % 4, (x + 2) % 4
    yu, yd, y2 = (y + 1) % 4, (y + 3) % 4, (y + 2) % 4
    e_out, e_in, e_opp = (p + 2 * zl + 3) % 4, (p + 5 - 2 * zl) % 4, (p + 2) % 4
    own = c * 4 + x
    right = (w, p * 4 + xr)
    left = (w, p * 4 + xl)
    core = (y * 4 + zl * 2 + oc, ex)
    z_out = (y * 4 + oz * 2 + c, e_out * 4 + x)
    z_in = (y * 4 + oz * 2 + c, ex)
    y_up = (yu * 4 + zl * 2 + c, ex)
    y_dn = (yd * 4 + zl * 2 + c, ex)
    zu, zd = (z + 1) % 8, (z + 7) % 8
    z_up = (y * 4 + (zu % 2) * 2 + c, (zu // 2) * 4 + x)
    z_dn = (y * 4 + (zd % 2) * 2 + c, (zd // 2) * 4 + x)

    def rc(i, src, dst, dev, group=0):
        return pltpu.make_async_remote_copy(
            src_ref=src, dst_ref=dst, send_sem=ssem.at[group], recv_sem=rsem.at[i],
            device_id=dev, device_id_type=MESH,
        )

    def send(i, src, dst, dev):
        rc(i, src, dst, dev, S_TOK if i < MS else S_W).start()

    def sent(group, ref):
        rc(0, ref, ref, core, group).wait_send()

    def arrived(i, dst):
        rc(i, dst, dst, core).wait_recv()

    loads = [
        pltpu.make_async_copy(gw.at[:, pl.ds(c * 128, 128)], W1.at[p, 0], lsem.at[0]),
        pltpu.make_async_copy(uw.at[:, pl.ds(c * 128, 128)], W1.at[p, 1], lsem.at[1]),
        pltpu.make_async_copy(dw.at[pl.ds(c * 128, 128)], WD.at[p], lsem.at[2]),
        pltpu.make_async_copy(tok, X.at[own], lsem.at[3]),
        pltpu.make_async_copy(tgt, TG, lsem.at[4]),
        pltpu.make_async_copy(meta, META.at[own], lsem.at[5]),
        pltpu.make_async_copy(meta, STEPS.at[w], lsem.at[6]),
    ]
    for load in (loads[1], loads[0], loads[2], *loads[3:]):
        load.start()

    barrier = pltpu.get_barrier_semaphore()

    def greet(dev):
        pl.semaphore_signal(barrier, inc=1, device_id=dev, device_id_type=MESH)

    def slot_dev(s):
        return (y * 4 + zl * 2 + s // 4, p * 4 + s % 4)

    for i in range(1, 8):
        greet(slot_dev((own + i) % 8))
    for i in range(1, 16):
        other = (w + i) % 16
        greet((other, ex))
    greet(z_out)
    pl.semaphore_wait(barrier, 23)

    A, B = pl.ds(0, HALF), pl.ds(HALF, HALF)
    send(T_RA, tok.at[A], X.at[own, A], right)
    send(T_LB, tok.at[B], X.at[own, B], left)
    send(T_RB, tok.at[B], X.at[own, B], right)
    send(T_LA, tok.at[A], X.at[own, A], left)
    send(T_C, tok, X.at[own], core)

    quarter = {0: 768, 1: 256, 6: 32}
    along_y = (0, 1, 6)

    def rows_of(e, k, first, count):
        if k == 0:
            return W1.at[e, 1, pl.ds(first, count)]
        if k == 1:
            return W1.at[e, 0, pl.ds(2048 + first, count)]
        if k < 6:
            return W1.at[e, 0, pl.ds(512 * (k - 2) + first, count)]
        if k == 6:
            return WD.at[e, pl.ds(first, count), pl.ds(0, 1536)]
        return WD.at[e, pl.ds(first, count), pl.ds(1536 + 768 * (k - 7), 768)]

    def chunk(e, k, q):
        return rows_of(e, k, quarter[k] * q, quarter[k])

    def half(e, k, q, h):
        n = quarter[k] // 2
        return rows_of(e, k, quarter[k] * q + n * h, n)

    def zchunk(e, k):
        if k in quarter:
            return chunk(e, k, y)
        return rows_of(e, k, 0, 512 if k < 6 else 128)

    def zhalf(e, k, h):
        if k in quarter:
            return half(e, k, y, h)
        n = 256 if k < 6 else 64
        return rows_of(e, k, n * h, n)

    def z1(k):
        send(Z1 + k, zchunk(p, k), zchunk(p, k), z_out)

    def z2(k):
        arrived(Z1 + k, zchunk(e_out, k))
        send(Z2 + k, zchunk(e_out, k), zchunk(e_out, k), z_in)

    def z3(k):
        arrived(Z2 + k, zchunk(e_in, k))
        send(Z3 + k, zhalf(e_in, k, oz), zhalf(e_in, k, oz), z_out)

    def z4(k):
        arrived(Z3 + k, zhalf(e_opp, k, zl))
        send(Z4 + k, zhalf(e_opp, k, zl), zhalf(e_opp, k, zl), z_in)

    def z5(k):
        arrived(Z4 + k, zhalf(e_opp, k, oz))

    es = (e_out, e_in, e_opp)

    def yid(n, k):
        return YQ + (n * 3 + along_y.index(k)) * 4

    def yq(n, k):
        i = yid(n, k)
        send(i, chunk(es[n], k, y), chunk(es[n], k, y), y_up)
        send(i + 1, chunk(es[n], k, y), chunk(es[n], k, y), y_dn)

    def yf(n, k):
        i = yid(n, k)
        arrived(i, chunk(es[n], k, yd))
        send(i + 2, half(es[n], k, yd, 0), half(es[n], k, yd, 0), y_up)
        arrived(i + 1, chunk(es[n], k, yu))
        send(i + 3, half(es[n], k, yu, 1), half(es[n], k, yu, 1), y_dn)

    def ye(n, k):
        i = yid(n, k)
        arrived(i + 2, half(es[n], k, y2, 0))
        arrived(i + 3, half(es[n], k, y2, 1))

    lane4 = lax.broadcasted_iota(jnp.int32, (512, 128), 1)

    def column(mb, r):
        rows = MXB[pl.ds(4 * mb, 4)].reshape(512, 128)
        return jnp.sum(jnp.where(lane4 == r, rows, 0.0), axis=1, keepdims=True)

    def forward(e):
        @pl.loop(0, 2)
        def _(mb):
            rows = X[pl.ds(4 * mb, 4)].reshape(512, D)
            weights = jnp.concatenate([W1[e, 0], W1[e, 1]], axis=1)
            pre = jnp.dot(rows, weights, preferred_element_type=F32)
            GU[e, mb] = pre
            gate, up = pre[:, :128], pre[:, 128:]
            mixed = gate * jax.nn.sigmoid(gate) * up * column(mb, e)
            at = (
                pl.ds(pl.multiple_of(512 * mb, 512), 512),
                pl.ds(pl.multiple_of(128 * e, 128), 128),
            )
            H[at] = mixed.astype(BF16)
            HS[at] = (mixed * column(mb, 4)).astype(BF16)

    loads[1].wait()
    z1(0)
    loads[0].wait()
    z1(1)
    z1(2)
    z1(3)
    loads[2].wait()

    @pl.loop(1, 8)
    def _(i):
        rc(MS, meta, META.at[own], slot_dev((own + i) % 8), S_META).start()

    @pl.loop(1, 16)
    def _(i):
        rc(MS, meta, STEPS.at[w], ((w + i) % 16, ex), S_META).start()

    z2(0)
    yq(0, 0)
    z2(1)
    yq(0, 1)
    arrived(T_RA, X.at[c * 4 + xl, A])
    send(T_FR, X.at[c * 4 + xl, A], X.at[c * 4 + xl, A], right)
    arrived(T_LB, X.at[c * 4 + xr, B])
    send(T_FL, X.at[c * 4 + xr, B], X.at[c * 4 + xr, B], left)
    z2(2)
    z3(0)
    yq(1, 0)
    z3(1)
    yq(1, 1)
    z1(4)
    z1(5)
    z2(3)
    yf(0, 0)
    z3(2)
    z4(0)
    yf(0, 1)
    z4(1)
    z3(3)
    z1(6)
    arrived(T_RB, X.at[c * 4 + xl, B])
    send(T_CL, X.at[c * 4 + xl], X.at[c * 4 + xl], core)
    arrived(T_LA, X.at[c * 4 + xr, A])
    send(T_CR, X.at[c * 4 + xr], X.at[c * 4 + xr], core)
    z5(0)
    yq(2, 0)
    z5(1)
    yq(2, 1)
    z2(4)
    yf(1, 0)
    z2(5)
    z4(2)
    z3(4)
    yf(1, 1)
    z4(3)
    z3(5)
    z2(6)
    yq(0, 6)
    arrived(T_FR, X.at[c * 4 + x2, A])
    arrived(T_FL, X.at[c * 4 + x2, B])
    send(T_CF, X.at[c * 4 + x2], X.at[c * 4 + x2], core)

    for load in loads[3:]:
        load.wait()

    arrived(MS, FS.at[0, pl.ds(0, 8 * 22)])

    lane = lax.broadcasted_iota(jnp.int32, (TOK, 128), 1)
    eye = lane == lax.broadcasted_iota(jnp.int32, (TOK, 128), 0)

    @pl.loop(0, 8)
    def _(s):
        rows = META[s]
        cols = jnp.zeros((TOK, 128), F32)
        for r in range(5):
            spread = jnp.where(eye, jnp.broadcast_to(rows[r : r + 1, :], (TOK, 128)), 0.0)
            cols = cols + jnp.where(lane == r, jnp.sum(spread, axis=1, keepdims=True), 0.0)
        MXB[s] = cols

    z3(6)
    yq(1, 6)
    z1(7)
    z1(8)
    arrived(T_C, X.at[oc * 4 + x])
    arrived(T_CL, X.at[oc * 4 + xl])
    arrived(T_CR, X.at[oc * 4 + xr])
    arrived(T_CF, X.at[oc * 4 + x2])
    forward(p)
    yf(2, 0)
    z4(4)
    z4(5)
    z4(6)
    z5(6)
    yq(2, 6)
    yf(2, 1)
    ye(0, 0)
    ye(0, 1)
    forward(e_out)
    yf(0, 6)
    ye(1, 0)
    ye(1, 1)
    forward(e_in)
    yf(1, 6)
    for k in range(2, 6):
        z5(k)
    ye(2, 0)
    ye(2, 1)
    forward(e_opp)
    yf(2, 6)
    z2(7)
    for n in range(3):
        ye(n, 6)

    G[...] = jnp.zeros_like(G)
    LS[...] = jnp.zeros_like(LS)

    def dcols(j):
        return pl.ds(pl.multiple_of(DC * j, DC), DC)

    def wd_cols(j):
        return WD[:, :, dcols(j)].reshape(512, DC)

    def hrows(who):
        return H[pl.ds(pl.multiple_of(512 * who, 512), 512), :]

    def s0(j):
        slot = j % 2

        @pl.when(j >= 2)
        def _():
            sent(S_PX + j - 2, PSD.at[slot])

        part = jnp.dot(hrows(oc), wd_cols(j), preferred_element_type=F32)
        PSD[slot] = part.astype(BF16).reshape(4, TOK, DC)
        rc(PX + j, PSD.at[slot], PRV.at[j], core, S_PX + j).start()

    def rs_copy(j, n):
        src = (
            PRV.at[j, x2, A], PRV.at[j, x2, B], PRV.at[j, xr, B], PRV.at[j, xl, A],
            PRV.at[j, xr, A], PRV.at[j, xl, B],
        )[n]
        return rc(RX + 6 * j + n, src, XR.at[j, n], right if n % 2 == 0 else left, S_RX)

    def s1(j):
        arrived(PX + j, PRV.at[j])
        part = jnp.dot(hrows(c), wd_cols(j), preferred_element_type=F32)
        both = part.reshape(4, TOK, DC) + PRV[j].astype(F32)
        PRV[j] = both.astype(BF16)
        for n in range(4):
            rs_copy(j, n).start()

    def add_into(ref, other):
        ref[...] = ref[...] + other[...]

    def s2(j):
        arrived(RX + 6 * j, XR.at[j, 0])
        add_into(PRV.at[j, xr, A], XR.at[j, 0])
        rs_copy(j, 4).start()
        arrived(RX + 6 * j + 1, XR.at[j, 1])
        add_into(PRV.at[j, xl, B], XR.at[j, 1])
        rs_copy(j, 5).start()

    def ag_copy(j, n):
        i = AG + 10 * j + n
        if n < 4:
            h = (A, B, B, A)[n]
            return rc(i, R.at[j, own, h], R.at[j, own, h], (right, left)[n % 2], S_AG)
        if n == 4:
            return rc(i, R.at[j, own], R.at[j, own], core, S_AG)
        if n == 5:
            return rc(i, R.at[j, c * 4 + xl, A], R.at[j, c * 4 + xl, A], right, S_AG)
        if n == 6:
            return rc(i, R.at[j, c * 4 + xr, B], R.at[j, c * 4 + xr, B], left, S_AG)
        s = c * 4 + (xl, xr, x2)[n - 7]
        return rc(i, R.at[j, s], R.at[j, s], core, S_AG)

    def ag_arrived(j, n):
        i = AG + 10 * j + n
        near = c * 4 + (xl if n in (0, 2) else xr)
        far = oc * 4
        dst = {
            0: R.at[j, near, A], 2: R.at[j, near, B], 1: R.at[j, near, B], 3: R.at[j, near, A],
            4: R.at[j, far + x], 5: R.at[j, c * 4 + x2, A], 6: R.at[j, c * 4 + x2, B],
            7: R.at[j, far + xl], 8: R.at[j, far + xr], 9: R.at[j, far + x2],
        }[n]
        arrived(i, dst)

    def s3(j):
        for n in (2, 3, 4, 5):
            arrived(RX + 6 * j + n, XR.at[j, n])
        base = PRV[j, x].astype(F32)
        top = base[:HALF] + XR[j, 4].astype(F32) + XR[j, 3].astype(F32)
        low = base[HALF:] + XR[j, 2].astype(F32) + XR[j, 5].astype(F32)
        mixed = jnp.concatenate([top, low], axis=0)
        resid = mixed - TG[:, dcols(j)].astype(F32)
        square = resid * resid
        folded = square[:, :128]
        for n in range(1, 6):
            folded = folded + square[:, 128 * n : 128 * (n + 1)]
        LS[...] += folded
        R[j, own] = resid.astype(BF16)
        for n in (0, 1, 2, 3, 4):
            ag_copy(j, n).start()

    def s4(j):
        ag_arrived(j, 0)
        ag_copy(j, 5).start()
        ag_arrived(j, 1)
        ag_copy(j, 6).start()
        ag_arrived(j, 2)
        ag_copy(j, 7).start()
        ag_arrived(j, 3)
        ag_copy(j, 8).start()

    def s5(j):
        ag_arrived(j, 5)
        ag_arrived(j, 6)
        ag_copy(j, 9).start()

    def piece(m, j, dest):
        return DM.at[m, dest // 2, j, dest % 2]

    def z_copy(q, m, j, step, way):
        i = ZR + 8 * q + 2 * step + way
        dest = (z + (4 - step if way == 0 else 4 + step)) % 8
        dev = z_up if way == 0 else z_dn
        if step == 0:
            return rc(i, piece(m, j, dest).at[A if way == 0 else B], ZH.at[q, way], dev, S_ZR + q)
        return rc(i, piece(m, j, dest), ZF.at[q, way, step - 1], dev, S_ZR + q)

    def z_start(q, m, j):
        z_copy(q, m, j, 0, 0).start()
        z_copy(q, m, j, 0, 1).start()

    def z_step(q, m, j, step):
        for way in range(2):
            i = ZR + 8 * q + 2 * (step - 1) + way
            dest = (z + (4 - step if way == 0 else 4 + step)) % 8
            if step == 1:
                arrived(i, ZH.at[q, way])
                add_into(piece(m, j, dest).at[A if way == 0 else B], ZH.at[q, way])
            else:
                arrived(i, ZF.at[q, way, step - 2])
                add_into(piece(m, j, dest), ZF.at[q, way, step - 2])
            z_copy(q, m, j, step, way).start()

    def z_sum(q, m, j):
        for way in range(2):
            arrived(ZR + 8 * q + 6 + way, ZF.at[q, way, 2])
        mine = piece(m, j, z)[...].astype(F32)
        return mine + ZF[q, 0, 2].astype(F32) + ZF[q, 1, 2].astype(F32)

    def z_end(q, m, j):
        total = z_sum(q, m, j)
        DM[m, p, j, zl] = total.astype(BF16)

    def s6(j):
        for n in (4, 7, 8, 9):
            ag_arrived(j, n)
        rows = R[j].reshape(1024, DC)
        down = lax.dot_general(HS[...], rows, (((0,), (0,)), ((), ())), preferred_element_type=F32)
        for e in range(4):
            for b in range(2):
                DM[2, e, j, b] = down[128 * e : 128 * (e + 1), DB * b : DB * (b + 1)].astype(BF16)
        z_start(j, 2, j)
        G[...] += lax.dot_general(
            rows, wd_cols(j), (((1,), (1,)), ((), ())), preferred_element_type=F32
        )

    stages = [s1, s2, s3, s4, s5, s6] + [
        functools.partial(lambda j, step: z_step(j, 2, j, step), step=step) for step in (1, 2, 3)
    ]

    late = {
        0: ((), (lambda: z3(7), lambda: z2(8))),
        1: ((), (lambda: z4(7), lambda: z3(8))),
        2: ((lambda: z5(7),), (lambda: z4(8),)),
        3: ((lambda: z5(8),), ()),
    }

    @pl.loop(0, 10)
    def _(t):
        for when, (before, _) in late.items():
            if before:

                @pl.when(t == when)
                def _():
                    for step in before:
                        step()

        @pl.when(t < 4)
        def _():
            s0(t)

        for when, (_, after) in late.items():
            if after:

                @pl.when(t == when)
                def _():
                    for step in after:
                        step()

        for n, stage in enumerate(stages):
            j = t - (n + 1)

            @pl.when((j >= 0) & (j < 4))
            def _():
                stage(j)

    sent(S_TOK, X.at[pl.ds(0, 7)])
    sent(S_W, DM.at[:, pl.ds(0, 3)])
    sent(S_META, FS.at[0, pl.ds(0, 8 * 22)])

    mean = jnp.sum(LS[...], axis=1, keepdims=True) * (0.5 / D)
    out[0, pl.ds(192, 1), pl.ds(0, TOK)] = jnp.sum(
        jnp.where(eye, mean, 0.0), axis=0, keepdims=True
    )

    @pl.loop(0, 8)
    def _(i):
        e, mb = i // 2, i % 2
        at = (pl.ds(pl.multiple_of(512 * mb, 512), 512), pl.ds(pl.multiple_of(128 * e, 128), 128))
        grad = G[at] * (column(mb, e) * column(mb, 4))
        pre = GU[e, mb]
        gate, up = pre[:, :128], pre[:, 128:]
        sig = jax.nn.sigmoid(gate)
        rows = at[0]
        GG[rows, pl.ds(pl.multiple_of(128 * e, 128), 128)] = (
            grad * up * (sig * (1.0 + gate * (1.0 - sig)))
        ).astype(BF16)
        GG[rows, pl.ds(pl.multiple_of(512 + 128 * e, 128), 128)] = (grad * (gate * sig)).astype(BF16)

    def dw_chunk(m, j):
        rows = X[:, :, dcols(j)].reshape(1024, DC)
        grads = lax.dot_general(
            GG[:, 512 * m : 512 * (m + 1)], rows, (((0,), (0,)), ((), ())),
            preferred_element_type=F32,
        )
        for e in range(4):
            for b in range(2):
                DM[m, e, j, b] = grads[128 * e : 128 * (e + 1), DB * b : DB * (b + 1)].astype(BF16)

    lo, hi = pl.ds(0, 2), pl.ds(2, 2)

    def yb_copy(n):
        src = (
            DM.at[0, lo, y2], DM.at[0, hi, y2], DM.at[0, hi, yu], DM.at[0, lo, yd],
            DM.at[0, lo, yu], DM.at[0, hi, yd],
        )[n]
        return rc(YB + n, src, YR1.at[n], y_up if n % 2 == 0 else y_dn, S_YB)

    def ys_copy(m, n):
        src = DM.at[m, p, (yu, yd, y2)[n], zl]
        dev = (y_up, y_dn, (y2 * 4 + zl * 2 + c, ex))[n]
        return rc(YS + 3 * (m - 1) + n, src, YR2.at[m - 1, n], dev, S_YS + m - 1)

    def yb_add(n, ref):
        arrived(YB + n, YR1.at[n])
        for a in range(2):
            for b in range(2):
                add_into(ref.at[a, b], YR1.at[n, a, b])

    def ys_start(m):
        for n in (2, 0, 1):
            ys_copy(m, n).start()

    def ys_sum(m):
        total = DM[m, p, y, zl].astype(F32)
        for n in (0, 1, 2):
            arrived(YS + 3 * (m - 1) + n, YR2.at[m - 1, n])
            total = total + YR2[m - 1, n].astype(F32)
        return total

    total_steps = jnp.sum(STEPS[...], axis=0)[4:5, :]
    mine_rows = pl.ds(pl.multiple_of(192 * c, 192), 192)
    other_rows = pl.ds(pl.multiple_of(192 * oc, 192), 192)

    def finish(m, total):
        FS[m] = total.T / total_steps
        rc(FX + m, FS.at[m, other_rows], FR.at[m], core, S_FX + m).start()

    def up_step(n, step):
        j = (y2, yu, yd, y)[n]
        if step == 0:
            z_start(4 + n, 1, j)
        elif step < 4:
            z_step(4 + n, 1, j, step)
        else:
            z_end(4 + n, 1, j)

    dw_chunk(0, y2)
    yb_copy(0).start()
    yb_copy(1).start()
    z_step(1, 2, 1, 3)
    z_step(2, 2, 2, 2)
    z_step(3, 2, 3, 1)
    dw_chunk(0, yu)
    yb_copy(2).start()
    dw_chunk(0, yd)
    yb_copy(3).start()
    dw_chunk(1, y2)
    up_step(0, 0)
    z_step(2, 2, 2, 3)
    z_step(3, 2, 3, 2)
    dw_chunk(1, yu)
    up_step(1, 0)
    dw_chunk(1, yd)
    up_step(2, 0)
    up_step(0, 1)
    z_step(3, 2, 3, 3)
    dw_chunk(1, y)
    up_step(3, 0)
    up_step(1, 1)
    yb_add(0, DM.at[0, lo, yu])
    yb_copy(4).start()
    yb_add(1, DM.at[0, hi, yd])
    yb_copy(5).start()
    up_step(0, 2)
    up_step(2, 1)
    dw_chunk(0, y)
    up_step(1, 2)
    up_step(3, 1)
    for j in range(4):
        z_end(j, 2, j)
    ys_start(2)
    up_step(0, 3)
    up_step(2, 2)
    up_step(1, 3)
    up_step(3, 2)
    yb_add(3, DM.at[0, lo, y])
    yb_add(2, DM.at[0, hi, y])
    up_step(2, 3)
    up_step(0, 4)
    up_step(3, 3)
    yb_add(4, DM.at[0, lo, y])
    yb_add(5, DM.at[0, hi, y])
    z_start(8, 0, y)
    up_step(1, 4)
    finish(2, ys_sum(2))
    up_step(2, 4)
    z_step(8, 0, y, 1)
    up_step(3, 4)
    ys_start(1)
    z_step(8, 0, y, 2)
    finish(1, ys_sum(1))
    z_step(8, 0, y, 3)
    finish(0, z_sum(8, 0, y))

    lanes = pl.ds(pl.multiple_of(128 * c, 128), 128)
    other_lanes = pl.ds(pl.multiple_of(128 * oc, 128), 128)
    for m in (2, 1, 0):
        out[m, pl.ds(0, 192), lanes] = FS[m, mine_rows]
        arrived(FX + m, FR.at[m])
        out[m, pl.ds(0, 192), other_lanes] = FR[m]

    for j in (2, 3):
        sent(S_PX + j, PSD.at[j % 2])
    sent(S_RX, DM.at[:, 0])
    sent(S_AG, X.at[pl.ds(0, 7)])
    for q in range(9):
        sent(S_ZR + q, W1.at[0, 0, pl.ds(0, 7 * 384)])
    sent(S_YB, DM.at[:, 0])
    for m in (1, 2):
        sent(S_YS + m - 1, YR2.at[m - 1])
    for m in range(3):
        sent(S_FX + m, FR.at[m])


def per_device(tokens, route_ids, route_mix, target, step_count, gate_weight, up_weight, down_weight):
    lines = jnp.arange(8, dtype=jnp.int32)[:, None, None]
    mix = jnp.sum(jnp.where(route_ids[None] == lines, route_mix[None], 0.0), axis=2)
    meta = jnp.where(lines[:, :, 0] == EXPERTS, step_count.astype(F32)[0], mix)
    any_spec = pl.BlockSpec(memory_space=pl.ANY)
    vmem_spec = pl.BlockSpec(memory_space=pltpu.VMEM)
    out = pl.pallas_call(
        kernel,
        out_shape=jax.ShapeDtypeStruct((3, 200, 256), F32),
        in_specs=[any_spec] * 6,
        out_specs=vmem_spec,
        scratch_shapes=[
            pltpu.VMEM((8, TOK, D), BF16),
            pltpu.VMEM((4, 2, D, 128), BF16),
            pltpu.VMEM((4, 128, D), BF16),
            pltpu.VMEM((4, 2, 512, 256), F32),
            pltpu.VMEM((1024, 512), BF16),
            pltpu.VMEM((1024, 512), BF16),
            pltpu.VMEM((8, TOK, 128), F32),
            pltpu.VMEM((8, 8, 128), F32),
            pltpu.VMEM((16, 8, 128), F32),
            pltpu.VMEM((4, 8, TOK, DC), BF16),
            pltpu.VMEM((2, 4, TOK, DC), BF16),
            pltpu.VMEM((4, 4, TOK, DC), BF16),
            pltpu.VMEM((4, 6, HALF, DC), BF16),
            pltpu.VMEM((TOK, D), BF16),
            pltpu.VMEM((1024, 512), F32),
            pltpu.VMEM((1024, 1024), BF16),
            pltpu.VMEM((3, 4, 4, 2, 128, DB), BF16),
            pltpu.VMEM((9, 2, HALF, DB), BF16),
            pltpu.VMEM((9, 2, 3, 128, DB), BF16),
            pltpu.VMEM((6, 2, 2, 128, DB), BF16),
            pltpu.VMEM((2, 3, 128, DB), BF16),
            pltpu.VMEM((3, DB, 128), F32),
            pltpu.VMEM((3, 192, 128), F32),
            pltpu.VMEM((TOK, 128), F32),
            pltpu.SemaphoreType.DMA((N_SEND,)),
            pltpu.SemaphoreType.DMA((N_SEM,)),
            pltpu.SemaphoreType.DMA((7,)),
        ],
        compiler_params=pltpu.CompilerParams(
            collective_id=0, has_side_effects=True, vmem_limit_bytes=67043328
        ),
    )(meta, tokens, target, gate_weight, up_weight, down_weight)
    return out[0, :192], out[1, :192], out[2, :192].T, out[0, 192, :TOK]


def solution(mesh):
    return jax.shard_map(
        per_device,
        mesh=mesh,
        in_specs=(
            P(("worker", "expert"), None),
            P(("worker", "expert"), None),
            P(("worker", "expert"), None),
            P(("worker", "expert"), None),
            P("worker"),
            P(None, "expert"),
            P(None, "expert"),
            P("expert", None),
        ),
        out_specs=(
            P("worker", "expert"),
            P("worker", "expert"),
            P("expert", "worker"),
            P(("worker", "expert")),
        ),
        check_vma=False,
    )
```

time: 216 us -> 205 us (0.949)
  Pallas kernels: 210 us -> 199 us
    pallas_call x1, Pallas kernels: 210 us -> 199 us  [per_device(): pl.pallas_call(kernel, out_shape=jax.ShapeDtypeStruct((3, 200, 256), F32)...]
where the time goes in v2:
time: 205 us
  Pallas kernels  199 us (97%)
  local copies, waits for them, and re-layouts  3.12 us (2%)
    pallas_call x1, Pallas kernels, per_device(): pl.pallas_call(kernel, out_shape=jax.ShapeDtypeStruct((3, 200, 256), F32)...  199 us

profile of v2, /device:TPU:1, one launch (start us, length us, event | category | flops | bytes accessed | tf_op | source)
XLA Modules:
  0.0 204.8 jit_solution(16942488817637822953)
XLA Ops:
  0.6 0.7 select_reduce_fusion
  2.0 0.7 broadcast_select_fusion.meta
  2.7 199.0 %shard_map.111 = f32[3,200,256]{2,1,0:T(8,128)} custom-call(f32[8,128]{1,0:T(8,128)} %broadcast_select_fusion.meta, bf16[128,3072]{1,0:T(8,128)(2,1)} %tok.1, bf16[128,3072]{1,0:T(8,128)(2,1)} %tgt.1, bf16[3072,256]{1,0:T(8,128)(2,1)} %gw.1, bf16[3072,256]{1,0:T(8,128)(2,1)} %uw.1, bf16[256,3072]{1,0:T(8,128)(2,1)} %dw.1), custom_call_target="tpu_custom_call" | custom-call | tf_op jit(solution)/shard_map/pallas_call | solution.py:693
  201.7 1.9 slice_bitcast_fusion
  203.6 1.2 slice_bitcast_fusion.3
  (1 shorter events, 0.0 us)

commit v3 on v2

--- a/solution.py
+++ b/solution.py
@@ -36,20 +36,20 @@
 PX = IDS.take(4)
 RX = IDS.take(24)
 AG = IDS.take(40)
-ZR = IDS.take(72)
-YB = IDS.take(6)
+ZR = IDS.take(80)
+YB = IDS.take(12)
 YS = IDS.take(6)
 FX = IDS.take(3)
 N_SEM = IDS.n
-S_TOK, S_W, S_META, S_RX, S_AG, S_YB, S_YS, S_PX, S_ZR, N_SEND = 0, 1, 2, 3, 4, 5, 6, 8, 12, 21
+S_TOK, S_W, S_META, S_RX, S_AG, S_YB, S_YS, S_PX, S_ZR, N_SEND = 0, 1, 2, 3, 4, 5, 7, 9, 13, 23
 S_FX = N_SEND
 N_SEND += 3
 
 
 def kernel(
     meta, tok, tgt, gw, uw, dw, out,
-    X, W1, WD, GU, H, HS, MXB, META, STEPS, R, PSD, PRV, XR, TG, G, GG, DM, ZH, ZF,
-    YR1, YR2, FS, FR, LS, ssem, rsem, lsem,
+    X, W1, WD, GU, H, HS, MXB, META, STEPS, R, PSD, PRV, XR, G, GG, DM, ZH, ZF,
+    YR1, YR2, YR3, FS, FR, LS, ssem, rsem, lsem,
 ):
     w = lax.axis_index("worker")
     ex = lax.axis_index("expert")
@@ -93,9 +93,11 @@
         pltpu.make_async_copy(uw.at[:, pl.ds(c * 128, 128)], W1.at[p, 1], lsem.at[1]),
         pltpu.make_async_copy(dw.at[pl.ds(c * 128, 128)], WD.at[p], lsem.at[2]),
         pltpu.make_async_copy(tok, X.at[own], lsem.at[3]),
-        pltpu.make_async_copy(tgt, TG, lsem.at[4]),
-        pltpu.make_async_copy(meta, META.at[own], lsem.at[5]),
-        pltpu.make_async_copy(meta, STEPS.at[w], lsem.at[6]),
+        pltpu.make_async_copy(meta, META.at[own], lsem.at[4]),
+        pltpu.make_async_copy(meta, STEPS.at[w], lsem.at[5]),
+    ] + [
+        pltpu.make_async_copy(tgt.at[:, pl.ds(DC * j, DC)], R.at[j, own], lsem.at[6 + j])
+        for j in range(4)
     ]
     for load in (loads[1], loads[0], loads[2], *loads[3:]):
         load.start()
@@ -410,7 +412,7 @@
         top = base[:HALF] + XR[j, 4].astype(F32) + XR[j, 3].astype(F32)
         low = base[HALF:] + XR[j, 2].astype(F32) + XR[j, 5].astype(F32)
         mixed = jnp.concatenate([top, low], axis=0)
-        resid = mixed - TG[:, dcols(j)].astype(F32)
+        resid = mixed - R[j, own].astype(F32)
         square = resid * resid
         folded = square[:, :128]
         for n in range(1, 6):
@@ -435,16 +437,35 @@
         ag_arrived(j, 6)
         ag_copy(j, 9).start()
 
-    def piece(m, j, dest):
-        return DM.at[m, dest // 2, j, dest % 2]
+    def span(q):
+        if isinstance(q, int) and 4 <= q < 8:
+            return 0, 96
+        return (96, 32) if isinstance(q, int) and q == 9 else (0, 128)
+
+    def piece(q, m, j, dest):
+        return DM.at[m, dest // 2, j, dest % 2, pl.ds(*span(q))]
+
+    def side(q, way):
+        count = span(q)[1] // 2
+        return pl.ds(count * way, count)
+
+    def zh(q, way):
+        if isinstance(q, int) and q == 9:
+            return ZH.at[4, way, pl.ds(48, 16)]
+        return ZH.at[q, way, pl.ds(0, span(q)[1] // 2)]
+
+    def zf(q, way, step):
+        if isinstance(q, int) and q == 9:
+            return ZF.at[4, way, step, pl.ds(96, 32)]
+        return ZF.at[q, way, step, pl.ds(0, span(q)[1])]
 
     def z_copy(q, m, j, step, way):
         i = ZR + 8 * q + 2 * step + way
         dest = (z + (4 - step if way == 0 else 4 + step)) % 8
         dev = z_up if way == 0 else z_dn
         if step == 0:
-            return rc(i, piece(m, j, dest).at[A if way == 0 else B], ZH.at[q, way], dev, S_ZR + q)
-        return rc(i, piece(m, j, dest), ZF.at[q, way, step - 1], dev, S_ZR + q)
+            return rc(i, piece(q, m, j, dest).at[side(q, way)], zh(q, way), dev, S_ZR + q)
+        return rc(i, piece(q, m, j, dest), zf(q, way, step - 1), dev, S_ZR + q)
 
     def z_start(q, m, j):
         z_copy(q, m, j, 0, 0).start()
@@ -455,22 +476,22 @@
             i = ZR + 8 * q + 2 * (step - 1) + way
             dest = (z + (4 - step if way == 0 else 4 + step)) % 8
             if step == 1:
-                arrived(i, ZH.at[q, way])
-                add_into(piece(m, j, dest).at[A if way == 0 else B], ZH.at[q, way])
+                arrived(i, zh(q, way))
+                add_into(piece(q, m, j, dest).at[side(q, way)], zh(q, way))
             else:
-                arrived(i, ZF.at[q, way, step - 2])
-                add_into(piece(m, j, dest), ZF.at[q, way, step - 2])
+                arrived(i, zf(q, way, step - 2))
+                add_into(piece(q, m, j, dest), zf(q, way, step - 2))
             z_copy(q, m, j, step, way).start()
 
     def z_sum(q, m, j):
         for way in range(2):
-            arrived(ZR + 8 * q + 6 + way, ZF.at[q, way, 2])
-        mine = piece(m, j, z)[...].astype(F32)
-        return mine + ZF[q, 0, 2].astype(F32) + ZF[q, 1, 2].astype(F32)
+            arrived(ZR + 8 * q + 6 + way, zf(q, way, 2))
+        mine = piece(q, m, j, z)[...].astype(F32)
+        return mine + zf(q, 0, 2)[...].astype(F32) + zf(q, 1, 2)[...].astype(F32)
 
     def z_end(q, m, j):
         total = z_sum(q, m, j)
-        DM[m, p, j, zl] = total.astype(BF16)
+        piece(q, m, j, z)[...] = total.astype(BF16)
 
     def s6(j):
         for n in (4, 7, 8, 9):
@@ -560,33 +581,46 @@
 
     lo, hi = pl.ds(0, 2), pl.ds(2, 2)
 
-    def yb_copy(n):
-        src = (
-            DM.at[0, lo, y2], DM.at[0, hi, y2], DM.at[0, hi, yu], DM.at[0, lo, yd],
-            DM.at[0, lo, yu], DM.at[0, hi, yd],
-        )[n]
-        return rc(YB + n, src, YR1.at[n], y_up if n % 2 == 0 else y_dn, S_YB)
+    def yb_part(n, m):
+        h = (lo, hi, hi, lo, lo, hi)[n]
+        to = (y2, y2, yu, yd, yu, yd)[n]
+        return yb_ref(h, to, m)
+
+    def yb_ref(h, to, m):
+        if m == 0:
+            return DM.at[0, h, to]
+        return DM.at[1, h, to, :, pl.ds(96, 32)]
+
+    def yb_copy(n, m=0):
+        dst = YR1.at[n] if m == 0 else YR3.at[n]
+        return rc(YB + 6 * m + n, yb_part(n, m), dst, y_up if n % 2 == 0 else y_dn, S_YB + m)
+
+    def ys_rows(m):
+        return pl.ds(0, 96 if m == 1 else 128)
 
     def ys_copy(m, n):
-        src = DM.at[m, p, (yu, yd, y2)[n], zl]
+        src = DM.at[m, p, (yu, yd, y2)[n], zl, ys_rows(m)]
         dev = (y_up, y_dn, (y2 * 4 + zl * 2 + c, ex))[n]
-        return rc(YS + 3 * (m - 1) + n, src, YR2.at[m - 1, n], dev, S_YS + m - 1)
-
-    def yb_add(n, ref):
-        arrived(YB + n, YR1.at[n])
+        return rc(YS + 3 * (m - 1) + n, src, YR2.at[m - 1, n, ys_rows(m)], dev, S_YS + m - 1)
+
+    def yb_add(n, h, to, m=0):
+        got = YR1 if m == 0 else YR3
+        arrived(YB + 6 * m + n, got.at[n])
+        ref = yb_ref(h, to, m)
         for a in range(2):
             for b in range(2):
-                add_into(ref.at[a, b], YR1.at[n, a, b])
+                add_into(ref.at[a, b], got.at[n, a, b])
 
     def ys_start(m):
         for n in (2, 0, 1):
             ys_copy(m, n).start()
 
     def ys_sum(m):
-        total = DM[m, p, y, zl].astype(F32)
+        rows = ys_rows(m)
+        total = DM[m, p, y, zl, rows].astype(F32)
         for n in (0, 1, 2):
-            arrived(YS + 3 * (m - 1) + n, YR2.at[m - 1, n])
-            total = total + YR2[m - 1, n].astype(F32)
+            arrived(YS + 3 * (m - 1) + n, YR2.at[m - 1, n, rows])
+            total = total + YR2[m - 1, n, rows].astype(F32)
         return total
 
     total_steps = jnp.sum(STEPS[...], axis=0)[4:5, :]
@@ -617,52 +651,68 @@
     dw_chunk(0, yd)
     yb_copy(3).start()
     dw_chunk(1, y2)
+    yb_copy(0, 1).start()
+    yb_copy(1, 1).start()
     up_step(0, 0)
     z_step(2, 2, 2, 3)
     z_step(3, 2, 3, 2)
     dw_chunk(1, yu)
+    yb_copy(2, 1).start()
     up_step(1, 0)
     dw_chunk(1, yd)
+    yb_copy(3, 1).start()
     up_step(2, 0)
+    yb_add(0, lo, yu)
+    yb_copy(4).start()
+    yb_add(1, hi, yd)
+    yb_copy(5).start()
     up_step(0, 1)
     z_step(3, 2, 3, 3)
     dw_chunk(1, y)
     up_step(3, 0)
     up_step(1, 1)
-    yb_add(0, DM.at[0, lo, yu])
-    yb_copy(4).start()
-    yb_add(1, DM.at[0, hi, yd])
-    yb_copy(5).start()
+    dw_chunk(0, y)
     up_step(0, 2)
     up_step(2, 1)
-    dw_chunk(0, y)
     up_step(1, 2)
     up_step(3, 1)
     for j in range(4):
         z_end(j, 2, j)
     ys_start(2)
+    yb_add(0, lo, yu, 1)
+    yb_copy(4, 1).start()
+    yb_add(1, hi, yd, 1)
+    yb_copy(5, 1).start()
     up_step(0, 3)
     up_step(2, 2)
     up_step(1, 3)
     up_step(3, 2)
-    yb_add(3, DM.at[0, lo, y])
-    yb_add(2, DM.at[0, hi, y])
+    yb_add(3, lo, y)
+    yb_add(2, hi, y)
+    yb_add(3, lo, y, 1)
+    yb_add(2, hi, y, 1)
     up_step(2, 3)
     up_step(0, 4)
+    yb_add(4, lo, y)
+    yb_add(5, hi, y)
+    z_start(8, 0, y)
     up_step(3, 3)
-    yb_add(4, DM.at[0, lo, y])
-    yb_add(5, DM.at[0, hi, y])
-    z_start(8, 0, y)
     up_step(1, 4)
+    yb_add(4, lo, y, 1)
+    yb_add(5, hi, y, 1)
+    z_start(9, 1, y)
+    z_step(8, 0, y, 1)
+    up_step(2, 4)
     finish(2, ys_sum(2))
-    up_step(2, 4)
-    z_step(8, 0, y, 1)
+    z_step(9, 1, y, 1)
+    z_step(8, 0, y, 2)
     up_step(3, 4)
     ys_start(1)
-    z_step(8, 0, y, 2)
-    finish(1, ys_sum(1))
+    z_step(9, 1, y, 2)
     z_step(8, 0, y, 3)
+    z_step(9, 1, y, 3)
     finish(0, z_sum(8, 0, y))
+    finish(1, jnp.concatenate([ys_sum(1), z_sum(9, 1, y)], axis=0))
 
     lanes = pl.ds(pl.multiple_of(128 * c, 128), 128)
     other_lanes = pl.ds(pl.multiple_of(128 * oc, 128), 128)
@@ -675,11 +725,12 @@
         sent(S_PX + j, PSD.at[j % 2])
     sent(S_RX, DM.at[:, 0])
     sent(S_AG, X.at[pl.ds(0, 7)])
-    for q in range(9):
-        sent(S_ZR + q, W1.at[0, 0, pl.ds(0, 7 * 384)])
+    for q in range(10):
+        sent(S_ZR + q, W1.at[0, 0, pl.ds(0, 21 * span(q)[1])])
     sent(S_YB, DM.at[:, 0])
+    sent(S_YB + 1, YR3)
     for m in (1, 2):
-        sent(S_YS + m - 1, YR2.at[m - 1])
+        sent(S_YS + m - 1, YR2.at[m - 1, :, ys_rows(m)])
     for m in range(3):
         sent(S_FX + m, FR.at[m])
 
@@ -709,7 +760,6 @@
             pltpu.VMEM((2, 4, TOK, DC), BF16),
             pltpu.VMEM((4, 4, TOK, DC), BF16),
             pltpu.VMEM((4, 6, HALF, DC), BF16),
-            pltpu.VMEM((TOK, D), BF16),
             pltpu.VMEM((1024, 512), F32),
             pltpu.VMEM((1024, 1024), BF16),
             pltpu.VMEM((3, 4, 4, 2, 128, DB), BF16),
@@ -717,12 +767,13 @@
             pltpu.VMEM((9, 2, 3, 128, DB), BF16),
             pltpu.VMEM((6, 2, 2, 128, DB), BF16),
             pltpu.VMEM((2, 3, 128, DB), BF16),
+            pltpu.VMEM((6, 2, 2, 32, DB), BF16),
             pltpu.VMEM((3, DB, 128), F32),
             pltpu.VMEM((3, 192, 128), F32),
             pltpu.VMEM((TOK, 128), F32),
             pltpu.SemaphoreType.DMA((N_SEND,)),
             pltpu.SemaphoreType.DMA((N_SEM,)),
-            pltpu.SemaphoreType.DMA((7,)),
+            pltpu.SemaphoreType.DMA((10,)),
         ],
         compiler_params=pltpu.CompilerParams(
             collective_id=0, has_side_effects=True, vmem_limit_bytes=67043328

time: 205 us -> 197 us (0.961)
  Pallas kernels: 199 us -> 191 us
    pallas_call x1, Pallas kernels: 199 us -> 191 us  [per_device(): pl.pallas_call(kernel, out_shape=jax.ShapeDtypeStruct((3, 200, 256), F32)...]
where the time goes in v3:
time: 197 us
  Pallas kernels  191 us (97%)
  local copies, waits for them, and re-layouts  3.12 us (2%)
    pallas_call x1, Pallas kernels, per_device(): pl.pallas_call(kernel, out_shape=jax.ShapeDtypeStruct((3, 200, 256), F32)...  191 us

profile of v3, /device:TPU:1, one launch (start us, length us, event | category | flops | bytes accessed | tf_op | source)
XLA Modules:
  0.0 196.6 jit_solution(10984580565540328357)
XLA Ops:
  0.6 0.7 select_reduce_fusion
  2.0 0.7 broadcast_select_fusion.meta
  2.7 190.8 %shard_map.111 = f32[3,200,256]{2,1,0:T(8,128)} custom-call(f32[8,128]{1,0:T(8,128)} %broadcast_select_fusion.meta, bf16[128,3072]{1,0:T(8,128)(2,1)} %tok.1, bf16[128,3072]{1,0:T(8,128)(2,1)} %tgt.1, bf16[3072,256]{1,0:T(8,128)(2,1)} %gw.1, bf16[3072,256]{1,0:T(8,128)(2,1)} %uw.1, bf16[256,3072]{1,0:T(8,128)(2,1)} %dw.1), custom_call_target="tpu_custom_call" | custom-call | tf_op jit(solution)/shard_map/pallas_call | solution.py:744
  193.5 1.9 slice_bitcast_fusion
  195.4 1.2 slice_bitcast_fusion.3
  (1 shorter events, 0.0 us)

commit v4 on v3

--- a/solution.py
+++ b/solution.py
@@ -539,7 +539,8 @@
                     for step in after:
                         step()
 
-        for n, stage in enumerate(stages):
+        for n in (1, 2, 3, 4, 0, 5, 6, 7, 8):
+            stage = stages[n]
             j = t - (n + 1)
 
             @pl.when((j >= 0) & (j < 4))

time: 197 us -> 197 us (level)
  no operation moved by 1% of the time
where the time goes in v4:
time: 197 us; the launch traced here: 196 us
  Pallas kernels  191 us (97%)
  local copies, waits for them, and re-layouts  3.12 us (2%)
    pallas_call x1, Pallas kernels, per_device(): pl.pallas_call(kernel, out_shape=jax.ShapeDtypeStruct((3, 200, 256), F32)...  191 us

profile of v4, /device:TPU:1, one launch (start us, length us, event | category | flops | bytes accessed | tf_op | source)
XLA Modules:
  0.0 196.5 jit_solution(11566251379341386274)
XLA Ops:
  0.6 0.7 select_reduce_fusion
  2.0 0.7 broadcast_select_fusion.meta
  2.7 190.7 %shard_map.111 = f32[3,200,256]{2,1,0:T(8,128)} custom-call(f32[8,128]{1,0:T(8,128)} %broadcast_select_fusion.meta, bf16[128,3072]{1,0:T(8,128)(2,1)} %tok.1, bf16[128,3072]{1,0:T(8,128)(2,1)} %tgt.1, bf16[3072,256]{1,0:T(8,128)(2,1)} %gw.1, bf16[3072,256]{1,0:T(8,128)(2,1)} %uw.1, bf16[256,3072]{1,0:T(8,128)(2,1)} %dw.1), custom_call_target="tpu_custom_call" | custom-call | tf_op jit(solution)/shard_map/pallas_call | solution.py:745
  193.4 1.9 slice_bitcast_fusion
  195.3 1.2 slice_bitcast_fusion.3
  (1 shorter events, 0.0 us)
